TPU v7x, 256 devices: a whole 4x4x8 slice. The times are simulated.
256 devices in a mesh: row: 32 (over x, z), col: 8 (over y, core).
Axes of the slice: x: 4, y: 4, z: 8, core: 2. Of those that a mesh axis runs over, the one named last changes fastest.
Arguments:
- front_tiles: bfloat16 [4, 8192, 2, 2048], P(None, 'row', None, 'col'), may hold values from -6 to 6
- fill_pattern: int32 [4, 32, 2, 8], P(None, 'row', None, 'col'), may hold values from 0 to 1
- w_inverse: bfloat16 [2, 256, 256], replicated, may hold values from -0.015625 to 0.015625
- samples: bfloat16 [4, 8192, 512], P(None, 'row'), may hold values from -6 to 6
Outputs:
- factor_slab: bfloat16 [4, 8192, 2, 2048], P(None, 'row', None, 'col')
- solved_rows: bfloat16 [4, 8192, 512], P(None, 'row')
All inputs are finite; a program needn't handle non-finite values.
Results may differ from a plain program's by a relative error of at most 0.0062.
Values may be sent and summed in bfloat16 or wider, within the bound.
No kernel may reach another device: no remote copies, remote signals or barrier semaphores. Data moves between devices by JAX's collectives and lax.ppermute only.
A program may use at most 64 MiB of HBM per device.

v0:
```python
import jax
import jax.numpy as jnp
from jax import lax
from jax.sharding import PartitionSpec as P


def broadcast(block, axis, holder):
    block = jnp.where(lax.axis_index(axis) == holder, block, jnp.zeros_like(block))
    return lax.psum(block, axis)


def share_rows(tiles, root):
    return broadcast(tiles, "col", root)


def share_samples(tiles, root):
    return broadcast(tiles, "row", root)


def column_tiles(rows, cols_here):
    row_count = lax.axis_size("row")
    col_count = lax.axis_size("col")
    col_pos = lax.axis_index("col")
    pieces = []
    for place in range(cols_here):
        wanted = place * col_count + col_pos
        holder = wanted % row_count
        local_at = wanted // row_count
        held_tile = lax.dynamic_index_in_dim(rows, local_at, 0, keepdims=False)
        pieces.append(broadcast(held_tile, "row", holder))
    return jnp.stack(pieces)


def body(front_tiles, fill_pattern, w_inverse, samples):
    rows_here = front_tiles.shape[0]
    cols_here = front_tiles.shape[2]
    row_count = lax.axis_size("row")
    row_pos = lax.axis_index("row")
    col_pos = lax.axis_index("col")
    tile_row = jnp.arange(rows_here) * row_count + row_pos
    pattern = fill_pattern.astype(jnp.bfloat16)
    masked = front_tiles * pattern
    own_first = masked[:, :, 0, :]
    first_cand = jnp.einsum(
        "akm,mn->akn", own_first, w_inverse[0], preferred_element_type=jnp.float32
    )
    first_cand = jnp.where(tile_row[:, None, None] >= 1, first_cand, 0.0).astype(jnp.bfloat16)
    first_panel = share_rows(first_cand, 0)
    first_cols = column_tiles(first_panel, cols_here)
    updated_second = own_first.astype(jnp.float32) - jnp.einsum(
        "akm,nm->akn", first_panel, first_cols[0], preferred_element_type=jnp.float32
    )
    updated_second = updated_second.astype(jnp.bfloat16)
    second_cand = jnp.einsum(
        "akm,mn->akn", updated_second, w_inverse[1], preferred_element_type=jnp.float32
    )
    second_cand = jnp.where(tile_row[:, None, None] >= 2, second_cand, 0.0).astype(jnp.bfloat16)
    second_panel = share_rows(second_cand, 1)
    second_cols = column_tiles(second_panel, cols_here)
    both_rows = jnp.concatenate([first_panel, second_panel], axis=2)
    both_cols = jnp.concatenate([first_cols, second_cols], axis=2)
    product = jnp.einsum("akm,bnm->akbn", both_rows, both_cols, preferred_element_type=jnp.float32)
    trailing = ((masked.astype(jnp.float32) - product) * pattern.astype(jnp.float32)).astype(
        jnp.bfloat16
    )
    first_lead = jnp.where(tile_row[:, None, None] >= 1, first_panel, own_first)
    second_lead = jnp.where(tile_row[:, None, None] >= 2, second_panel, updated_second)
    lead_tiles = jnp.where(
        col_pos == 0, first_lead, jnp.where(col_pos == 1, second_lead, trailing[:, :, 0, :])
    )
    factor_slab = trailing.at[:, :, 0, :].set(lead_tiles)
    first_local = jnp.einsum(
        "mn,ms->ns", w_inverse[0], samples[0], preferred_element_type=jnp.float32
    )
    first_solve = share_samples(first_local.astype(jnp.bfloat16), 0)
    reduced = (
        samples[0].astype(jnp.float32)
        - jnp.dot(first_panel[0], first_solve, preferred_element_type=jnp.float32)
    ).astype(jnp.bfloat16)
    second_local = jnp.einsum(
        "mn,ms->ns", w_inverse[1], reduced, preferred_element_type=jnp.float32
    )
    second_solve = share_samples(second_local.astype(jnp.bfloat16), 1)
    stacked = jnp.concatenate([first_solve, second_solve], axis=0)
    remaining = samples.astype(jnp.float32) - jnp.einsum(
        "akm,ms->aks", both_rows, stacked, preferred_element_type=jnp.float32
    )
    remaining = remaining.astype(jnp.bfloat16)
    top_rows = jnp.where(
        row_pos == 0, first_solve, jnp.where(row_pos == 1, second_solve, remaining[0])
    )
    solved_rows = remaining.at[0].set(top_rows)
    return (factor_slab, solved_rows)


def solution(mesh):
    in_specs = (P(None, "row", None, "col"), P(None, "row", None, "col"), P(), P(None, "row", None))
    out_specs = (P(None, "row", None, "col"), P(None, "row", None))
    return jax.shard_map(body, mesh=mesh, in_specs=in_specs, out_specs=out_specs, check_vma=False)
```

profile of v0, /device:TPU:8, one launch (start us, length us, event | category | flops | bytes accessed | tf_op | source)
XLA Modules:
  0.0 465.0 jit_solution(3660325440382189734)
XLA Ops:
  7.2 0.0 all-reduce.7.cloned.1.call-start
  7.2 0.7 convert_element_type.41
  7.9 0.0 copy-start.8
  7.9 1.4 copy_multiply_fusion
  9.4 0.0 copy-done.8
  9.4 0.0 copy-start.6
  9.4 1.1 fusion.4
  10.5 0.0 all-reduce.7.cloned.1.call-update
  10.5 0.0 all-reduce.13.cloned.1.call-start
  10.6 0.0 copy-done.6
  10.6 1.0 fusion.6
  11.6 66.2 %all-reduce.7.cloned.1.call-done = bf16[4,256,256]{2,1,0:T(8,128)(2,1)} async-done(((bf16[4,256,256]{2,1,0:T(8,128)(2,1)}), bf16[4,256,256]{2,1,0:T(8,128)(2,1)}) %all-reduce.7.cloned.1.call-update) | async-done | bytes 524304 | tf_op jit(solution)/shard_map/psum | solution.py:9
  77.8 0.0 copy-start
  77.8 1.8 dynamic-slice_select_fusion.2
  79.5 0.0 all-reduce.13.cloned.1.call-update
  79.6 0.0 all-reduce.9.cloned.1.call-start
  79.6 150.6 %all-reduce.13.cloned.1.call-done = (bf16[256,256]{1,0:T(8,128)(2,1)}, bf16[256,512]{1,0:T(8,128)(2,1)}) async-done(((bf16[256,256]{1,0:T(8,128)(2,1)}, bf16[256,512]{1,0:T(8,128)(2,1)}), (bf16[256,256]{1,0:T(8,128)(2,1)}, bf16[256,512]{1,0:T(8,128)(2,1)})) %all-reduce.13.cloned.1.call-update) | async-done | bytes 393232 | tf_op jit(solution)/shard_map/psum | solution.py:9
  230.3 0.0 copy-done
  230.3 1.2 fusion
  231.5 0.0 copy-start.2
  231.5 2.0 fusion.3
  233.6 0.0 all-reduce.9.cloned.1.call-update
  233.6 0.0 all-reduce.11.cloned.1.call-start
  233.6 0.0 copy-done.2
  233.6 2.1 fusion.8
  235.7 59.4 %all-reduce.9.cloned.1.call-done = bf16[4,256,256]{2,1,0:T(8,128)(2,1)} async-done(((bf16[4,256,256]{2,1,0:T(8,128)(2,1)}), bf16[4,256,256]{2,1,0:T(8,128)(2,1)}) %all-reduce.9.cloned.1.call-update) | async-done | bytes 524304 | tf_op jit(solution)/shard_map/psum | solution.py:9
  295.1 0.0 copy-start.1
  295.1 1.8 dynamic-slice_select_fusion.1
  296.9 0.0 all-reduce.11.cloned.1.call-update
  296.9 0.0 copy-start.4
  296.9 0.8 constant_dynamic-update-slice_fusion.1
  297.7 0.0 copy-done.1
  297.7 0.8 constant_dynamic-update-slice_fusion
  298.6 152.2 %all-reduce.11.cloned.1.call-done = (bf16[1,256,256]{2,1,0:T(8,128)(2,1)}, bf16[1,256,256]{2,1,0:T(8,128)(2,1)}, bf16[1,256,256]{2,1,0:T(8,128)(2,1)}, bf16[256,512]{1,0:T(8,128)(2,1)}) async-done(((bf16[1,256,256]{2,1,0:T(8,128)(2,1)}, bf16[1,256,256]{2,1,0:T(8,128)(2,1)}, bf16[1,256,256]{2,1,0:T(8,128)(2,1)}, bf16[256,512]{1,0:T(8,128)(2,1)}), (bf16[1,256,256]{2,1,0:T(8,128)(2,1)}, ...) | async-done | bytes 655376 | tf_op jit(solution)/shard_map/psum | solution.py:9
  450.7 0.0 copy-done.4
  450.7 2.1 multiply_convert_fusion
  452.8 0.6 fusion.13
  453.4 0.0 copy-start.3
  453.4 0.0 copy-start.7
  453.4 2.0 copy.9
  455.5 0.0 copy-done.3
  455.5 0.0 copy-done.7
  455.5 1.9 subtract_convert_fusion
  457.4 0.1 fusion.26
  457.5 0.0 copy-start.5
  457.6 1.0 copy-done.5
  (3 shorter events, 0.0 us)
Async XLA Ops:
  7.2 70.6 %all-reduce.7.cloned.1.call-start = ((), (), s32[]{:S(2)}) async-start(), calls=%async_computation | async-start | bytes 1048576 | tf_op jit(solution)/shard_map/psum | solution.py:9
  7.9 1.4 copy-start.8
  9.4 1.2 copy-start.6
  10.5 219.8 %all-reduce.13.cloned.1.call-start = ((), (), s32[]{:S(2)}) async-start(), calls=%async_computation.3 | async-start | bytes 786432 | tf_op jit(solution)/shard_map/psum | solution.py:9
  77.8 152.5 %copy-start = (bf16[4,256,256]{2,1,0:T(8,128)(2,1)S(1)}, bf16[4,256,256]{2,1,0:T(8,128)(2,1)}, u32[]{:S(2)}) copy-start(bf16[4,256,256]{2,1,0:T(8,128)(2,1)} %all-reduce.7.cloned.1.call-done) | copy-start | bytes 1572868
  79.6 215.6 %all-reduce.9.cloned.1.call-start = ((), (), s32[]{:S(2)}) async-start(), calls=%async_computation.1 | async-start | bytes 1048576 | tf_op jit(solution)/shard_map/psum | solution.py:9
  231.5 2.1 copy-start.2
  233.6 217.2 %all-reduce.11.cloned.1.call-start = ((), (), s32[]{:S(2)}) async-start(), calls=%async_computation.2 | async-start | bytes 1310720 | tf_op jit(solution)/shard_map/psum | solution.py:9
  295.1 2.6 copy-start.1
  296.9 153.9 %copy-start.4 = (bf16[256,256]{1,0:T(8,128)(2,1)S(1)}, bf16[256,256]{1,0:T(8,128)(2,1)}, u32[]{:S(2)}) copy-start(bf16[256,256]{1,0:T(8,128)(2,1)} %get-tuple-element.32) | copy-start | bytes 393220
  453.4 2.1 copy-start.3
  453.4 2.1 copy-start.7
  457.5 1.0 copy-start.5
Sparse Core Ops, SparseCore 0:
  10.9 66.8 all-reduce.6
  81.9 148.3 all-reduce.12
  233.7 61.3 all-reduce.8
  299.3 151.3 all-reduce.10
where the time goes:
time: 465 us
  waiting for transfers between devices  429 us (92%)
  between operations  13.9 us (3%)
  matrix products  11.4 us (2%)
  other arithmetic  6.38 us (1%)
  local copies, waits for them, and re-layouts  4.71 us (1%)
    psum x4, waiting for transfers between devices, broadcast(): return lax.psum(block, axis)  428 us
  transfers between devices with their start and end apart: 4, of which 4 were waited for; matrix products, arithmetic and copies ran while one was open for 1% of the time, Pallas kernels for 0%

commit v1 on v0

--- a/solution.py
+++ b/solution.py
@@ -6,7 +6,7 @@
 
 def broadcast(block, axis, holder):
     block = jnp.where(lax.axis_index(axis) == holder, block, jnp.zeros_like(block))
-    return lax.psum(block, axis)
+    return jnp.sum(lax.all_gather(block, axis), axis=0)
 
 
 def share_rows(tiles, root):

time: 465 us -> 642 us (1.38)
  waiting for transfers between devices: 429 us -> 573 us
  other arithmetic: 6.38 us -> 33.2 us
  local copies, waits for them, and re-layouts: 4.71 us -> 12.7 us
    all_gather x0 -> x8, waiting for transfers between devices: none -> 571 us  [broadcast(): return jnp.sum(lax.all_gather(block, axis), axis=0)]
    psum x4 -> x0, waiting for transfers between devices: 428 us -> none  [broadcast(): return lax.psum(block, axis)]
    reduce_sum x0 -> x8, other arithmetic: none -> 28.9 us  [broadcast(): return jnp.sum(lax.all_gather(block, axis), axis=0)]
    unnamed x20 -> x8, local copies, waits for them, and re-layouts: 3.88 us -> 12.6 us
  transfers between devices with their start and end apart: 4 -> 8, of which waited for: 4 -> 8; matrix products, arithmetic and copies ran while one was open for 1% -> 4% of each run, Pallas kernels for 0% -> 0%
where the time goes in v1:
time: 642 us; the launch traced here: 641 us
  waiting for transfers between devices  573 us (89%)
  other arithmetic  33.2 us (5%)
  between operations  14.3 us (2%)
  local copies, waits for them, and re-layouts  12.7 us (2%)
  matrix products  8.02 us (1%)
    all_gather x8, waiting for transfers between devices, broadcast(): return jnp.sum(lax.all_gather(block, axis), axis=0)  571 us
    reduce_sum x8, other arithmetic, broadcast(): return jnp.sum(lax.all_gather(block, axis), axis=0)  28.9 us
  transfers between devices with their start and end apart: 8, of which 8 were waited for; matrix products, arithmetic and copies ran while one was open for 4% of the time, Pallas kernels for 0%

profile of v1, /device:TPU:8, one launch (start us, length us, event | category | flops | bytes accessed | tf_op | source)
XLA Modules:
  0.0 641.3 jit_solution(4651787603233146712)
XLA Ops:
  7.2 0.0 all-gather.21.cloned.1.call-start
  7.2 0.7 convert_element_type.27
  8.0 1.4 copy_multiply_fusion
  9.4 1.1 fusion.4
  10.4 0.0 all-gather.21.cloned.1.call-update
  10.5 0.0 all-gather.13.cloned.1.call-start
  10.6 36.5 %all-gather.21.cloned.1.call-done = bf16[32,256,256]{2,1,0:T(8,128)(2,1)} async-done(((bf16[4,256,256]{2,1,0:T(8,128)(2,1)}), bf16[32,256,256]{2,1,0:T(8,128)(2,1)}) %all-gather.21.cloned.1.call-update) | async-done | bytes 4194320 | tf_op jit(solution)/shard_map/all_gather | solution.py:9
  47.1 2.8 reduce_sum.100
  50.0 0.7 dynamic-slice_select_fusion.2
  50.7 0.0 all-gather.13.cloned.1.call-update
  50.7 0.0 all-gather.23.cloned.1.call-start
  50.8 82.8 %all-gather.13.cloned.1.call-done = bf16[32,256,256]{2,1,0:T(8,128)(2,1)} async-done(((bf16[1,256,256]{2,1,0:T(8,128)(2,1)}), bf16[32,256,256]{2,1,0:T(8,128)(2,1)}) %all-gather.13.cloned.1.call-update) | async-done | bytes 4194320 | tf_op jit(solution)/shard_map/all_gather | solution.py:9
  133.6 2.8 reduce_sum.101
  136.4 0.3 fusion
  136.7 1.1 fusion.3
  137.8 0.0 all-gather.23.cloned.1.call-update
  137.8 0.0 all-gather.25.cloned.1.call-start
  137.9 1.9 fusion.6
  139.8 0.0 all-gather.25.cloned.1.call-update
  139.8 0.0 all-gather.15.cloned.1.call-start
  139.8 0.5 all-gather.15.cloned.1.call-update
  140.4 0.0 all-gather.17.cloned.1.call-start
  140.4 27.9 %all-gather.23.cloned.1.call-done = bf16[32,256,256]{2,1,0:T(8,128)(2,1)} async-done(((bf16[4,256,256]{2,1,0:T(8,128)(2,1)}), bf16[32,256,256]{2,1,0:T(8,128)(2,1)}) %all-gather.23.cloned.1.call-update) | async-done | bytes 4194320 | tf_op jit(solution)/shard_map/all_gather | solution.py:9
  168.3 2.8 reduce_sum.102
  171.2 0.7 dynamic-slice_select_fusion.1
  171.9 0.0 all-gather.17.cloned.1.call-update
  171.9 0.0 all-gather.19.cloned.1.call-start
  172.0 0.7 all-gather.19.cloned.1.call-update
  172.7 0.2 all-gather.27.cloned.1.call-start
  172.9 97.2 %all-gather.25.cloned.1.call-done = bf16[8192,512]{1,0:T(8,128)(2,1)} async-done(((bf16[256,512]{1,0:T(8,128)(2,1)}), bf16[8192,512]{1,0:T(8,128)(2,1)}) %all-gather.25.cloned.1.call-update) | async-done | bytes 8388624 | tf_op jit(solution)/shard_map/all_gather | solution.py:9
  270.2 4.8 reduce_sum.106
  274.9 2.2 fusion.8
  277.1 74.3 %all-gather.15.cloned.1.call-done = bf16[32,256,256]{2,1,0:T(8,128)(2,1)} async-done(((bf16[1,256,256]{2,1,0:T(8,128)(2,1)}), bf16[32,256,256]{2,1,0:T(8,128)(2,1)}) %all-gather.15.cloned.1.call-update) | async-done | bytes 4194320 | tf_op jit(solution)/shard_map/all_gather | solution.py:9
  351.4 2.8 reduce_sum.103
  354.2 78.2 %all-gather.17.cloned.1.call-done = bf16[32,256,256]{2,1,0:T(8,128)(2,1)} async-done(((bf16[1,256,256]{2,1,0:T(8,128)(2,1)}), bf16[32,256,256]{2,1,0:T(8,128)(2,1)}) %all-gather.17.cloned.1.call-update) | async-done | bytes 4194320 | tf_op jit(solution)/shard_map/all_gather | solution.py:9
  432.4 2.8 reduce_sum.104
  435.2 78.3 %all-gather.19.cloned.1.call-done = bf16[32,256,256]{2,1,0:T(8,128)(2,1)} async-done(((bf16[1,256,256]{2,1,0:T(8,128)(2,1)}), bf16[32,256,256]{2,1,0:T(8,128)(2,1)}) %all-gather.19.cloned.1.call-update) | async-done | bytes 4194320 | tf_op jit(solution)/shard_map/all_gather | solution.py:9
  513.5 2.8 reduce_sum.105
  516.3 0.7 multiply_convert_fusion
  517.1 0.5 fusion.13
  517.6 2.0 copy.13
  519.7 95.9 %all-gather.27.cloned.1.call-done = bf16[8192,512]{0,1:T(8,128)(2,1)} async-done(((bf16[256,512]{0,1:T(8,128)(2,1)}), bf16[8192,512]{0,1:T(8,128)(2,1)}) %all-gather.27.cloned.1.call-update) | async-done | bytes 8388624 | tf_op jit(solution)/shard_map/all_gather | solution.py:9
  615.6 9.5 %copy.17 = bf16[64,8,32,256]{3,2,1,0:T(8,128)(2,1)} copy(bf16[64,8,32,256]{3,1,2,0:T(8,128)(2,1)} %bitcast.83) | data formatting | bytes 16777216
  625.2 7.3 %bitcast_reduce_fusion = bf16[256,512]{0,1:T(8,128)(2,1)S(1)} fusion(bf16[64,8,32,256]{3,2,1,0:T(8,128)(2,1)} %copy.17), kind=kLoop, calls=%fused_computation | loop fusion | flops 4063232 | bytes 8650752 | tf_op jit(solution)/shard_map/reduce_sum | solution.py:9
  632.4 0.1 copy.11
  632.6 0.7 subtract_convert_fusion
  633.3 0.1 fusion.24
  633.5 1.0 copy-done
  (9 shorter events, 0.1 us)
Async XLA Ops:
  7.2 2.2 copy-start.2
  7.2 39.9 %all-gather.21.cloned.1.call-start = ((), (), s32[]{:S(2)}) async-start(), calls=%async_computation.4 | async-start | bytes 4718592 | tf_op jit(solution)/shard_map/all_gather | solution.py:9
  10.5 123.1 %all-gather.13.cloned.1.call-start = ((), (), s32[]{:S(2)}) async-start(), calls=%async_computation | async-start | bytes 4325376 | tf_op jit(solution)/shard_map/all_gather | solution.py:9
  50.7 117.6 %all-gather.23.cloned.1.call-start = ((), (), s32[]{:S(2)}) async-start(), calls=%async_computation.5 | async-start | bytes 4718592 | tf_op jit(solution)/shard_map/all_gather | solution.py:9
  137.8 132.4 %all-gather.25.cloned.1.call-start = ((), (), s32[]{:S(2)}) async-start(), calls=%async_computation.6 | async-start | bytes 8650752 | tf_op jit(solution)/shard_map/all_gather | solution.py:9
  139.8 211.7 %all-gather.15.cloned.1.call-start = ((), (), s32[]{:S(2)}) async-start(), calls=%async_computation.1 | async-start | bytes 4325376 | tf_op jit(solution)/shard_map/all_gather | solution.py:9
  140.4 292.0 %all-gather.17.cloned.1.call-start = ((), (), s32[]{:S(2)}) async-start(), calls=%async_computation.2 | async-start | bytes 4325376 | tf_op jit(solution)/shard_map/all_gather | solution.py:9
  171.9 341.6 %all-gather.19.cloned.1.call-start = ((), (), s32[]{:S(2)}) async-start(), calls=%async_computation.3 | async-start | bytes 4325376 | tf_op jit(solution)/shard_map/all_gather | solution.py:9
  172.7 442.9 %all-gather.27.cloned.1.call-start = ((), (), s32[]{:S(2)}) async-start(), calls=%async_computation.7 | async-start | bytes 8650752 | tf_op jit(solution)/shard_map/all_gather | solution.py:9
  625.2 7.4 %copy-start.1 = (bf16[4,256,512]{2,1,0:T(8,128)(2,1)S(1)}, bf16[4,256,512]{2,1,0:T(8,128)(2,1)}, u32[]{:S(2)}) copy-start(bf16[4,256,512]{2,1,0:T(8,128)(2,1)} %param.11) | copy-start | bytes 3145732
  633.5 1.0 copy-start
Sparse Core Ops, SparseCore 0:
  10.6 36.4 all-gather.20
  50.8 82.6 all-gather.12
  137.9 30.3 all-gather.22
  171.4 98.7 all-gather.24
  272.6 78.7 all-gather.14
  353.9 78.4 all-gather.16
  435.0 78.4 all-gather.18
  516.6 99.0 all-gather.26
